TPU v7x, 32 devices: a whole 2x2x4 slice. The times are simulated.
32 devices in a mesh: freq: 2 (over x), atom: 16 (over z, y, core).
Axes of the slice: x: 2, y: 2, z: 4, core: 2. Of those that a mesh axis runs over, the one named last changes fastest.
Arguments:
- ham_diag: float32 [2, 128, 128], replicated
- ham_coup: float32 [1, 128, 128], replicated, may hold values from -0.25 to 0.25
- neighbors: int32 [256, 64], replicated, may hold values from 0 to 127, as said below
- pair_count: int32 [256], replicated, may hold values from 16 to 64
- shifts: int32 [8], replicated, may hold values from 1 to 16
- g_pairs: float32 [2, 32, 16384], P(None, ('freq', 'atom')), may hold values from -3 to 3
- emit_coup: float32 [2, 8, 16384], replicated, may hold values from -0.09375 to 0.09375
- absorb_coup: float32 [2, 8, 16384], replicated, may hold values from -0.09375 to 0.09375
Outputs:
- green: float32 [2, 32, 2, 128, 128], P(None, ('freq', 'atom'))
Inputs may be any that keep to these rules, and one draw needn't show every extreme that they name: `neighbors`: entry 0 of each row is the atom's own index within its slab (atom index modulo 128); the entries of a row are distinct.
All inputs are finite; a program needn't handle non-finite values.
Results may differ from a plain program's by a relative error of at most 0.0001.
Values sent between devices are 32-bit elements; how exact they have to be, the bound alone decides.
No kernel may reach another device: no remote copies, remote signals or barrier semaphores. Data moves between devices by JAX's collectives and lax.ppermute only.
A program may use at most 128 MiB of HBM per device.

v0:
```python
import jax
import jax.numpy as jnp
from jax import lax
from jax.sharding import PartitionSpec as P

ORB = 128
SLABS = 2
NBR = 64
MODES = 8
HALO = 16
INV_STEPS = 22
BROADEN = 0.8
ENERGY_LOW = -2.5
ENERGY_SPAN = 5.0


def with_halo(cells, sides, width):
    for axis, dim in sides:
        count = lax.axis_size(axis)
        ends = count - 1
        head = lax.slice_in_dim(cells, 0, width, axis=dim)
        tail = lax.slice_in_dim(cells, cells.shape[dim] - width, cells.shape[dim], axis=dim)
        cells = jnp.concatenate(
            [
                lax.ppermute(tail, axis, [(i, (i + 1) % count) for i in range(ends)]),
                cells,
                lax.ppermute(head, axis, [((i + 1) % count, i) for i in range(ends)]),
            ],
            axis=dim,
        )
    return cells


def matmul(left, right):
    return jnp.dot(left, right, precision=lax.Precision.HIGHEST, preferred_element_type=jnp.float32)


def complex_product(left, right):
    first = matmul(left[0], right[0])
    second = matmul(left[1], right[1])
    third = matmul(left[0] + left[1], right[0] + right[1])
    return (first - second, third - first - second)


def sandwich(outer_left, inner, outer_right):
    return (
        matmul(matmul(outer_left, inner[0]), outer_right),
        matmul(matmul(outer_left, inner[1]), outer_right),
    )


def invert(real_part, imag_part):
    order = real_part.shape[0]
    unit_matrix = jnp.eye(order, dtype=real_part.dtype)
    scale = 1.0 / (jnp.sum(real_part * real_part) + jnp.sum(imag_part * imag_part))
    start = (real_part.T * scale, -imag_part.T * scale)

    def newton_step(index, current):
        product = complex_product((real_part, imag_part), current)
        residue = (2.0 * unit_matrix - product[0], -product[1])
        return complex_product(current, residue)

    return lax.fori_loop(0, INV_STEPS, newton_step, start)


def slab_green(sigma_blocks, energy, ham_diag, ham_coup):
    slabs = ham_diag.shape[0]
    order = ham_diag.shape[1]
    unit_matrix = jnp.eye(order, dtype=ham_diag.dtype)
    diag_real = [
        energy * unit_matrix - ham_diag[slab_index] - sigma_blocks[0, slab_index]
        for slab_index in range(slabs)
    ]
    diag_imag = [BROADEN * unit_matrix - sigma_blocks[1, slab_index] for slab_index in range(slabs)]
    right_parts = [None] * slabs
    right_parts[slabs - 1] = invert(diag_real[slabs - 1], diag_imag[slabs - 1])
    slab_index = 0
    coupling = ham_coup[slab_index]
    folded = sandwich(coupling, right_parts[slab_index + 1], coupling.T)
    right_parts[slab_index] = invert(
        diag_real[slab_index] - folded[0], diag_imag[slab_index] - folded[1]
    )
    blocks = [right_parts[0]]
    slab_index = 1
    coupling = ham_coup[slab_index - 1]
    carried = sandwich(coupling.T, blocks[-1], coupling)
    own_part = right_parts[slab_index]
    update = complex_product(complex_product(own_part, carried), own_part)
    blocks.append((own_part[0] + update[0], own_part[1] + update[1]))
    return jnp.stack(
        [jnp.stack([entry[0] for entry in blocks]), jnp.stack([entry[1] for entry in blocks])]
    )


def sigma_blocks_of(sigma_pairs, neighbors, live):
    values = sigma_pairs.reshape(2, SLABS, ORB, NBR) * live
    slab_ids = jnp.broadcast_to(
        jnp.arange(SLABS, dtype=jnp.int32)[:, None, None], (SLABS, ORB, NBR)
    )
    row_ids = jnp.broadcast_to(jnp.arange(ORB, dtype=jnp.int32)[None, :, None], (SLABS, ORB, NBR))
    columns = neighbors.reshape(SLABS, ORB, NBR)
    empty = jnp.zeros((2, SLABS, ORB, ORB), sigma_pairs.dtype)
    return empty.at[:, slab_ids, row_ids, columns].add(values)


def convolve(source, base, length, shifts, emit_coup, absorb_coup):
    width = source.shape[2]
    real_sum = jnp.zeros((length, width), source.dtype)
    imag_sum = jnp.zeros((length, width), source.dtype)
    for mode_index in range(MODES):
        shift_now = shifts[mode_index]
        below = lax.dynamic_slice_in_dim(source, base - shift_now, length, 1)
        above = lax.dynamic_slice_in_dim(source, base + shift_now, length, 1)
        emit_real = emit_coup[0, mode_index][None, :]
        emit_imag = emit_coup[1, mode_index][None, :]
        absorb_real = absorb_coup[0, mode_index][None, :]
        absorb_imag = absorb_coup[1, mode_index][None, :]
        real_sum = (
            real_sum
            + emit_real * below[0]
            - emit_imag * below[1]
            + absorb_real * above[0]
            - absorb_imag * above[1]
        )
        imag_sum = (
            imag_sum
            + emit_real * below[1]
            + emit_imag * below[0]
            + absorb_real * above[1]
            + absorb_imag * above[0]
        )
    return jnp.stack([real_sum, imag_sum])


def on_device(ham_diag, ham_coup, neighbors, pair_count, shifts, g_pairs, emit_coup, absorb_coup):
    e_dev = g_pairs.shape[1]
    atom_count = lax.axis_size("atom")
    group = e_dev * atom_count
    energy_total = group * lax.axis_size("freq")
    freq_index = lax.axis_index("freq")
    atom_index = lax.axis_index("atom")
    live = (
        (jnp.arange(NBR, dtype=jnp.int32)[None, :] < pair_count[:, None])
        .astype(jnp.float32)
        .reshape(SLABS, ORB, NBR)
    )
    first_energy = (freq_index * atom_count + atom_index) * e_dev

    def solve_one(sigma_pairs, energy):
        return slab_green(sigma_blocks_of(sigma_pairs, neighbors, live), energy, ham_diag, ham_coup)

    owned = lax.all_to_all(g_pairs, "atom", split_axis=2, concat_axis=1, tiled=True)
    owned_width = owned.shape[2]
    own_emit = lax.dynamic_slice_in_dim(emit_coup, atom_index * owned_width, owned_width, 2)
    own_absorb = lax.dynamic_slice_in_dim(absorb_coup, atom_index * owned_width, owned_width, 2)
    source = with_halo(owned, (("freq", 1),), HALO)
    sigma = convolve(source, HALO, group, shifts, own_emit, own_absorb)
    returned = lax.all_to_all(sigma, "atom", split_axis=1, concat_axis=2, tiled=True)

    def single(pieces):
        return solve_one(pieces[0], pieces[1])

    positions = (first_energy + jnp.arange(e_dev, dtype=jnp.int32)).astype(jnp.float32)
    solved = lax.map(
        single, (jnp.moveaxis(returned, 1, 0), ENERGY_LOW + ENERGY_SPAN * positions / energy_total)
    )
    return jnp.moveaxis(solved, 0, 1)


def solution(mesh):
    return jax.shard_map(
        on_device,
        mesh=mesh,
        in_specs=(P(), P(), P(), P(), P(), P(None, ("freq", "atom"), None), P(), P()),
        out_specs=P(None, ("freq", "atom"), None, None, None),
        check_vma=False,
    )
```

profile of v0, /device:TPU:0, one launch (start us, length us, event | category | flops | bytes accessed | tf_op | source)
XLA Modules:
  0.0 409.6 jit_solution(11434350478482396900)
XLA Ops:
  0.0 14.7 %copy.80 = f32[2,1,16384]{0,1,2:T(1,128)} copy(f32[2,1,16384]{2,1,0:T(1,128)} %param.17) | data formatting | bytes 262144 | tf_op args[5]
  14.7 0.5 broadcast.412
  15.2 74.4 %reduce.4 = f32[16384,2]{1,0:T(8,128)} reduce(f32[16384,1,2]{2,1,0:T(1,128)} %bitcast.233, f32[]{:T(128)} %broadcast.412), dimensions={1}, to_apply=%bitcast.153.reduce_sub_computation | reduce | bytes 262148
  89.6 8.3 %reshape.561 = f32[16,1,2048]{2,1,0:T(1,128)} reshape(f32[16384,2]{1,0:T(8,128)} %reduce.4) | data formatting | bytes 262144
  97.9 7.4 %all-to-all-start = ((f32[16,1,2048]{2,1,0:T(1,128)}), f32[16,1,2048]{2,1,0:T(1,128)S(1)}, u32[]{:S(2)}, u32[]{:S(2)}) async-start(f32[16,1,2048]{2,1,0:T(1,128)} %reshape.561), calls=%async_computation | async-start | bytes 262144 | tf_op jit(solution)/shard_map/all_to_all | solution.py:152
  105.3 0.7 fusion.62
  126.2 2.0 constant_dynamic-slice_fusion.1
  128.6 0.9 reduce.5
  129.4 14.7 %reshape.562 = f32[16384,1,2]{2,1,0:T(1,128)} reshape(f32[16,2048]{1,0:T(8,128)S(1)} %reduce.5) | data formatting | bytes 262144
  144.2 5.2 %copy.95 = f32[2,16,1024]{2,1,0:T(8,128)S(1)} copy(f32[2,16,1024]{0,2,1:T(8,128)} %bitcast.234) | data formatting | bytes 262144 | tf_op jit(solution)/shard_map/all_to_all | solution.py:152
  149.4 1.3 collective-permute-start.1
  150.7 4.6 %collective-permute-start = (f32[2,16,1024]{2,1,0:T(8,128)S(1)}, f32[2,16,1024]{2,1,0:T(8,128)S(1)}, u32[]{:S(2)}, u32[]{:S(2)}) collective-permute-start(f32[2,16,1024]{2,1,0:T(8,128)S(1)} %copy.95), channel_id=1, source_target_pairs={{0,16},{1,17},{2,18},{3,19},{4,20},{5,21},{6,22},{7,23},{8,24},{9,... | collective-permute-start | bytes 393224 | tf_op jit(solution)/shard_map/ppermute | solution.py:25
  155.5 1.7 collective-permute-done.1
  157.2 1.2 collective-permute-done
  158.4 0.6 multiply_subtract_fusion
  159.0 0.6 multiply_add_fusion
  159.6 0.8 copy.82
  160.4 5.8 %all-to-all-start.1 = ((f32[2,16,1024]{2,0,1:T(2,128)}), f32[2,16,1024]{2,0,1:T(2,128)S(1)}, u32[]{:S(2)}, u32[]{:S(2)}) async-start(f32[2,16,1024]{2,0,1:T(2,128)} %copy.82), calls=%async_computation.1 | async-start | bytes 262144 | tf_op jit(solution)/shard_map/all_to_all | solution.py:158
  166.5 7.5 %all-to-all-done.1 = f32[2,16,1024]{2,0,1:T(2,128)S(1)} async-done(((f32[2,16,1024]{2,0,1:T(2,128)}), f32[2,16,1024]{2,0,1:T(2,128)S(1)}, u32[]{:S(2)}, u32[]{:S(2)}) %all-to-all-start.1) | async-done | bytes 131104 | tf_op jit(solution)/shard_map/all_to_all | solution.py:158
  174.2 4.8 %copy.96 = f32[2,128,64,2]{3,2,1,0:T(8,128)} copy(f32[2,128,64,2]{2,1,0,3:T(8,128)S(1)} %multiply_bitcast_fusion) | data formatting | bytes 262144 | tf_op jit(solution)/shard_map/while/body/eval_jaxpr/mul | solution.py:96
  179.0 94.4 %scatter_custom_fusion = f32[2,32768]{0,1:T(8,128)} fusion(s32[16384]{0:T(1024)S(1)} %reshape.553, f32[16384,2]{1,0:T(8,128)} %bitcast.235, f32[]{:T(128)} %constant.119.clone.1), kind=kCustom, calls=%fused_computation.37 | custom fusion | flops 32768 | bytes 262656
  273.4 27.8 %fusion.60 = (f32[1,1,128,128]{0,3,2,1:T(8,128)}, f32[1,1,128,128]{0,3,2,1:T(8,128)}, f32[1,1,128,128]{0,3,2,1:T(8,128)}, f32[1,1,128,128]{0,3,2,1:T(8,128)}) fusion(f32[2,2,128,128]{0,3,2,1:T(8,128)} %bitcast.232), kind=kLoop, calls=%fused_computation.120 | loop fusion | bytes 524288 | tf_op jit(solution)/shard_map/while/body/eval_jaxpr/slice | solution.py:74
  301.2 5.2 %copy.100 = f32[1,1,128,128]{3,2,1,0:T(8,128)S(1)} copy(f32[1,1,128,128]{0,3,2,1:T(8,128)} %get-tuple-element.218) | data formatting | bytes 131072
  306.4 5.2 %copy.99 = f32[1,1,128,128]{3,2,1,0:T(8,128)S(1)} copy(f32[1,1,128,128]{0,3,2,1:T(8,128)} %get-tuple-element.219) | data formatting | bytes 131072
  311.6 0.6 select_subtract_fusion.7
  312.3 0.7 multiply_reduce_fusion.4
  314.4 38.5 %while.40 = (s32[]{:T(128)}, f32[128,128]{0,1:T(8,128)S(1)}, f32[128,128]{0,1:T(8,128)S(1)}, f32[128,128]{1,0:T(8,128)S(1)}, f32[128,128]{1,0:T(8,128)S(1)}, /*index=5*/f32[128,128]{1,0:T(8,128)S(1)}, s32[]{:T(128)}) while((s32[]{:T(128)}, f32[128,128]{0,1:T(8,128)S(1)}, f32[128,128]{0,1:T(8,128)S(1)}, f32[128,128]{1,0:T(8,128)S(1)}, ...), condition=%wide.region_4.5_spmd.clone, body=%wide.region_3.4_spmd.clone.sunk | while | flops 151273472 | bytes 2162765 | solution.py:63
  315.8 0.3 fusion.148
  326.3 0.3 fusion.148
  328.1 0.3 fusion.148
  329.8 0.3 fusion.148
  331.6 0.3 fusion.148
  333.3 0.3 fusion.148
  335.1 0.3 fusion.148
  336.8 0.3 fusion.148
  338.6 0.3 fusion.148
  340.3 0.3 fusion.148
  342.1 0.3 fusion.148
  343.8 0.3 fusion.148
  345.6 0.3 fusion.148
  347.3 0.3 fusion.148
  349.1 0.3 fusion.148
  353.7 5.2 %copy.101 = f32[1,1,128,128]{3,2,1,0:T(8,128)S(1)} copy(f32[1,1,128,128]{0,3,2,1:T(8,128)} %get-tuple-element.217) | data formatting | bytes 131072
  358.9 5.2 %copy.98 = f32[1,1,128,128]{3,2,1,0:T(8,128)S(1)} copy(f32[1,1,128,128]{0,3,2,1:T(8,128)} %get-tuple-element.220) | data formatting | bytes 131072
  364.1 1.0 multiply_reduce_fusion.1
  365.1 0.9 multiply_reduce_fusion.2
  367.4 38.5 %while.41 = (s32[]{:T(128)}, f32[128,128]{0,1:T(8,128)S(1)}, f32[128,128]{0,1:T(8,128)S(1)}, f32[128,128]{1,0:T(8,128)S(1)}, f32[128,128]{1,0:T(8,128)S(1)}, /*index=5*/f32[128,128]{1,0:T(8,128)S(1)}, s32[]{:T(128)}) while((s32[]{:T(128)}, f32[128,128]{0,1:T(8,128)S(1)}, f32[128,128]{0,1:T(8,128)S(1)}, f32[128,128]{1,0:T(8,128)S(1)}, ...), condition=%wide.region_8.9_spmd.clone, body=%wide.region_7.8_spmd.clone.sunk | while | flops 151273472 | bytes 2162765 | solution.py:63
  368.8 0.3 fusion.164
  370.6 0.3 fusion.164
  372.3 0.3 fusion.164
  374.1 0.3 fusion.164
  375.8 0.3 fusion.164
  386.3 0.3 fusion.164
  388.1 0.3 fusion.164
  389.8 0.3 fusion.164
  391.6 0.3 fusion.164
  393.3 0.3 fusion.164
  395.1 0.3 fusion.164
  396.8 0.3 fusion.164
  398.6 0.3 fusion.164
  400.3 0.3 fusion.164
  402.1 0.3 fusion.164
  403.8 0.3 fusion.164
  408.9 0.7 maximum_bitcast_fusion
  (373 shorter events, 70.1 us)
Async XLA Ops:
  0.0 353.0 %copy-start = (f32[1,128,128]{2,1,0:T(8,128)S(1)}, f32[1,128,128]{2,1,0:T(8,128)}, u32[]{:S(2)}) copy-start(f32[1,128,128]{2,1,0:T(8,128)} %param.13) | copy-start | bytes 196612
  89.6 15.7 %copy-start.3 = (s32[8]{0:T(128)S(1)}, s32[8]{0:T(128)}, u32[]{:S(2)}) copy-start(s32[8]{0:T(128)} %param.16) | copy-start | bytes 100
  89.6 36.4 %copy-start.2 = (s32[256,64]{0,1:T(8,128)S(1)}, s32[256,64]{0,1:T(8,128)}, u32[]{:S(2)}) copy-start(s32[256,64]{0,1:T(8,128)} %param.14) | copy-start | bytes 196612
  89.6 38.7 %copy-start.6 = (s32[3]{0:T(128)S(1)}, s32[3]{0:T(128)}, u32[]{:S(2)}) copy-start(s32[3]{0:T(128)} %constant.131) | copy-start | bytes 40
  97.9 30.7 %all-to-all-start = ((f32[16,1,2048]{2,1,0:T(1,128)}), f32[16,1,2048]{2,1,0:T(1,128)S(1)}, u32[]{:S(2)}, u32[]{:S(2)}) async-start(f32[16,1,2048]{2,1,0:T(1,128)} %reshape.561), calls=%async_computation | async-start | bytes 262144 | tf_op jit(solution)/shard_map/all_to_all | solution.py:152
  129.4 25.9 %copy-start.5 = (s32[3]{0:T(128)S(1)}, s32[3]{0:T(128)}, u32[]{:S(2)}) copy-start(s32[3]{0:T(128)} %constant.128) | copy-start | bytes 40
  144.2 22.2 %copy-start.4 = (s32[256]{0:T(256)S(1)}, s32[256]{0:T(256)}, u32[]{:S(2)}) copy-start(s32[256]{0:T(256)} %param.15) | copy-start | bytes 3076
  149.4 7.7 %collective-permute-start.1 = (f32[2,16,1024]{2,1,0:T(8,128)S(1)}, f32[2,16,1024]{2,1,0:T(8,128)S(1)}, u32[]{:S(2)}, u32[]{:S(2)}) collective-permute-start(f32[2,16,1024]{2,1,0:T(8,128)S(1)} %copy.95), channel_id=1, source_target_pairs={{16,0},{17,1},{18,2},{19,3},{20,4},{21,5},{22,6},{23,7},{24,8},{25... | collective-permute-start | bytes 393224 | tf_op jit(solution)/shard_map/ppermute | solution.py:27
  150.7 7.6 %collective-permute-start = (f32[2,16,1024]{2,1,0:T(8,128)S(1)}, f32[2,16,1024]{2,1,0:T(8,128)S(1)}, u32[]{:S(2)}, u32[]{:S(2)}) collective-permute-start(f32[2,16,1024]{2,1,0:T(8,128)S(1)} %copy.95), channel_id=1, source_target_pairs={{0,16},{1,17},{2,18},{3,19},{4,20},{5,21},{6,22},{7,23},{8,24},{9,... | collective-permute-start | bytes 393224 | tf_op jit(solution)/shard_map/ppermute | solution.py:25
  160.4 13.7 %all-to-all-start.1 = ((f32[2,16,1024]{2,0,1:T(2,128)}), f32[2,16,1024]{2,0,1:T(2,128)S(1)}, u32[]{:S(2)}, u32[]{:S(2)}) async-start(f32[2,16,1024]{2,0,1:T(2,128)} %copy.82), calls=%async_computation.1 | async-start | bytes 262144 | tf_op jit(solution)/shard_map/all_to_all | solution.py:158
  301.2 10.5 %copy-start.1 = (f32[2,128,128]{2,1,0:T(8,128)S(1)}, f32[2,128,128]{2,1,0:T(8,128)}, u32[]{:S(2)}) copy-start(f32[2,128,128]{2,1,0:T(8,128)} %param.12) | copy-start | bytes 393220
where the time goes:
time: 412 us; the launch traced here: 410 us
  other arithmetic  174 us (42%)
  local copies, waits for them, and re-layouts  102 us (25%)
  matrix products  79.1 us (19%)
  between operations  23.3 us (6%)
  starting transfers between devices  19 us (5%)
  waiting for transfers between devices  10.4 us (3%)
    unnamed x5, other arithmetic  169 us
    dot_general x278, matrix products, matmul(): jnp.dot(left, right, precision=lax.Precision.HIGHEST, preferred_element_t...  79.1 us
    unnamed x24, local copies, waits for them, and re-layouts  59.3 us
    slice x1, local copies, waits for them, and re-layouts, slab_green(): sigma_blocks[1, slab_index]  27.8 us
  transfers between devices with their start and end apart: 4, of which 3 were waited for; matrix products, arithmetic and copies ran while one was open for 1% of the time, Pallas kernels for 0%

commit v1 on v0

--- a/solution.py
+++ b/solution.py
@@ -149,7 +149,13 @@
     def solve_one(sigma_pairs, energy):
         return slab_green(sigma_blocks_of(sigma_pairs, neighbors, live), energy, ham_diag, ham_coup)
 
-    owned = lax.all_to_all(g_pairs, "atom", split_axis=2, concat_axis=1, tiled=True)
+    trails_enter = lambda point, dim_k, in_dim: jnp.concatenate(
+        lax.all_to_all(
+            jnp.stack(jnp.split(point, lax.psum(1, "atom"), axis=dim_k), axis=0), "atom", 0, 0
+        ),
+        axis=in_dim,
+    )
+    owned = trails_enter(g_pairs, 2, 1)
     owned_width = owned.shape[2]
     own_emit = lax.dynamic_slice_in_dim(emit_coup, atom_index * owned_width, owned_width, 2)
     own_absorb = lax.dynamic_slice_in_dim(absorb_coup, atom_index * owned_width, owned_width, 2)

time: 412 us -> 304 us (0.74)
  other arithmetic: 174 us -> 99.7 us
  local copies, waits for them, and re-layouts: 102 us -> 70.9 us
    unnamed x5 -> x4, other arithmetic: 169 us -> 96.2 us
    unnamed x24 -> x27, local copies, waits for them, and re-layouts: 59.3 us -> 30.1 us
    all_to_all x1, local copies, waits for them, and re-layouts: 5.23 us -> 0.05 us  [on_device(): lax.all_to_all(jnp.stack(jnp.split(point, lax.psum(1, 'atom'), axis=dim_k...]
  transfers between devices with their start and end apart: 4 -> 4, of which waited for: 3 -> 3; matrix products, arithmetic and copies ran while one was open for 1% -> 2% of each run, Pallas kernels for 0% -> 0%
where the time goes in v1:
time: 304 us; the launch traced here: 303 us
  other arithmetic  99.7 us (33%)
  matrix products  79 us (26%)
  local copies, waits for them, and re-layouts  70.9 us (23%)
  between operations  23 us (8%)
  starting transfers between devices  18.8 us (6%)
  waiting for transfers between devices  9.6 us (3%)
    unnamed x4, other arithmetic  96.2 us
    dot_general x278, matrix products, matmul(): jnp.dot(left, right, precision=lax.Precision.HIGHEST, preferred_element_t...  79 us
    unnamed x27, local copies, waits for them, and re-layouts  30.1 us
    slice x1, local copies, waits for them, and re-layouts, slab_green(): sigma_blocks[1, slab_index]  27.8 us
    all_to_all x1, waiting for transfers between devices, on_device(): lax.all_to_all(sigma, 'atom', split_axis=1, concat_axis=2, tiled=True)  7.52 us
    all_to_all x1, starting transfers between devices, on_device(): lax.all_to_all(jnp.stack(jnp.split(point, lax.psum(1, 'atom'), axis=dim_k...  7.41 us
  transfers between devices with their start and end apart: 4, of which 3 were waited for; matrix products, arithmetic and copies ran while one was open for 2% of the time, Pallas kernels for 0%

profile of v1, /device:TPU:0, one launch (start us, length us, event | category | flops | bytes accessed | tf_op | source)
XLA Modules:
  0.0 303.3 jit_solution(3694903082982405307)
XLA Ops:
  0.0 0.9 fusion.61
  0.9 0.6 constant_dynamic-update-slice_fusion.15
  1.5 0.6 constant_dynamic-update-slice_fusion.14
  2.1 0.6 constant_dynamic-update-slice_fusion.13
  2.7 0.6 constant_dynamic-update-slice_fusion.12
  3.3 0.6 constant_dynamic-update-slice_fusion.11
  3.9 0.6 constant_dynamic-update-slice_fusion.10
  4.5 0.6 constant_dynamic-update-slice_fusion.9
  5.1 0.6 constant_dynamic-update-slice_fusion.8
  5.7 0.6 constant_dynamic-update-slice_fusion.7
  6.3 0.6 constant_dynamic-update-slice_fusion.6
  6.9 0.6 constant_dynamic-update-slice_fusion.5
  7.5 0.6 constant_dynamic-update-slice_fusion.4
  8.1 0.6 constant_dynamic-update-slice_fusion.3
  8.7 0.6 constant_dynamic-update-slice_fusion.2
  9.3 0.6 constant_dynamic-update-slice_fusion.1
  9.9 0.6 constant_dynamic-update-slice_fusion
  10.5 7.4 %all-to-all-start = ((f32[16,2,1,1024]{3,1,2,0:T(2,128)}), f32[16,2,1,1024]{3,1,2,0:T(2,128)S(1)}, u32[]{:S(2)}, u32[]{:S(2)}) async-start(f32[16,2,1,1024]{3,1,2,0:T(2,128)} %constant_dynamic-update-slice_fusion), calls=%async_computation | async-start | bytes 262144 | tf_op jit(solution)/shard_map/all_to_all | solution.py:153
  18.0 1.6 fusion.63
  39.6 0.9 reshape.550
  40.7 2.2 constant_dynamic-slice_fusion.1
  43.0 0.9 and_reduce_fusion
  44.0 1.3 collective-permute-start.1
  45.3 4.6 %collective-permute-start = (f32[2,16,1024]{2,1,0:T(8,128)S(1)}, f32[2,16,1024]{2,1,0:T(8,128)S(1)}, u32[]{:S(2)}, u32[]{:S(2)}) collective-permute-start(f32[2,16,1024]{2,1,0:T(8,128)S(1)} %bitcast.301), channel_id=1, source_target_pairs={{0,16},{1,17},{2,18},{3,19},{4,20},{5,21},{6,22},{7,23},{8,24},{9,... | collective-permute-start | bytes 393224 | tf_op jit(solution)/shard_map/ppermute | solution.py:25
  49.8 0.9 multiply_reduce_fusion
  50.7 0.9 collective-permute-done.1
  51.6 1.2 collective-permute-done
  52.8 0.6 multiply_subtract_fusion
  53.4 0.6 multiply_add_fusion
  54.0 0.8 copy.90
  54.8 5.5 %all-to-all-start.1 = ((f32[2,16,1024]{2,0,1:T(2,128)}), f32[2,16,1024]{2,0,1:T(2,128)S(1)}, u32[]{:S(2)}, u32[]{:S(2)}) async-start(f32[2,16,1024]{2,0,1:T(2,128)} %copy.90), calls=%async_computation.1 | async-start | bytes 262144 | tf_op jit(solution)/shard_map/all_to_all | solution.py:164
  60.7 7.5 %all-to-all-done.1 = f32[2,16,1024]{2,0,1:T(2,128)S(1)} async-done(((f32[2,16,1024]{2,0,1:T(2,128)}), f32[2,16,1024]{2,0,1:T(2,128)S(1)}, u32[]{:S(2)}, u32[]{:S(2)}) %all-to-all-start.1) | async-done | bytes 131104 | tf_op jit(solution)/shard_map/all_to_all | solution.py:164
  68.4 4.8 %copy.103 = f32[2,128,64,2]{3,2,1,0:T(8,128)} copy(f32[2,128,64,2]{2,1,0,3:T(8,128)S(1)} %multiply_bitcast_fusion) | data formatting | bytes 262144 | tf_op jit(solution)/shard_map/while/body/eval_jaxpr/mul | solution.py:96
  73.2 94.4 %scatter_custom_fusion = f32[2,32768]{0,1:T(8,128)} fusion(s32[16384]{0:T(1024)S(1)} %reshape.558, f32[16384,2]{1,0:T(8,128)} %bitcast.299, f32[]{:T(128)} %constant.119.clone.1), kind=kCustom, calls=%fused_computation.37 | custom fusion | flops 32768 | bytes 262656
  167.5 27.8 %fusion.60 = (f32[1,1,128,128]{0,3,2,1:T(8,128)}, f32[1,1,128,128]{0,3,2,1:T(8,128)}, f32[1,1,128,128]{0,3,2,1:T(8,128)}, f32[1,1,128,128]{0,3,2,1:T(8,128)}) fusion(f32[2,2,128,128]{0,3,2,1:T(8,128)} %bitcast.298), kind=kLoop, calls=%fused_computation.153 | loop fusion | bytes 524288 | tf_op jit(solution)/shard_map/while/body/eval_jaxpr/slice | solution.py:74
  195.3 5.2 %copy.123 = f32[1,1,128,128]{3,2,1,0:T(8,128)S(1)} copy(f32[1,1,128,128]{0,3,2,1:T(8,128)} %get-tuple-element.218) | data formatting | bytes 131072
  200.6 5.2 %copy.122 = f32[1,1,128,128]{3,2,1,0:T(8,128)S(1)} copy(f32[1,1,128,128]{0,3,2,1:T(8,128)} %get-tuple-element.219) | data formatting | bytes 131072
  205.8 0.6 select_subtract_fusion.7
  206.4 0.6 multiply_reduce_fusion.4
  208.3 38.5 %while.40 = (s32[]{:T(128)}, f32[128,128]{0,1:T(8,128)S(1)}, f32[128,128]{0,1:T(8,128)S(1)}, f32[128,128]{1,0:T(8,128)S(1)}, f32[128,128]{1,0:T(8,128)S(1)}, /*index=5*/f32[128,128]{1,0:T(8,128)S(1)}, s32[]{:T(128)}) while((s32[]{:T(128)}, f32[128,128]{0,1:T(8,128)S(1)}, f32[128,128]{0,1:T(8,128)S(1)}, f32[128,128]{1,0:T(8,128)S(1)}, ...), condition=%wide.region_4.5_spmd.clone, body=%wide.region_3.4_spmd.clone.sunk | while | flops 151273472 | bytes 2162765 | solution.py:63
  209.8 0.3 fusion.149
  211.5 0.3 fusion.149
  213.3 0.3 fusion.149
  215.0 0.3 fusion.149
  216.8 0.3 fusion.149
  227.3 0.3 fusion.149
  229.0 0.3 fusion.149
  230.8 0.3 fusion.149
  232.5 0.3 fusion.149
  234.3 0.3 fusion.149
  236.0 0.3 fusion.149
  237.8 0.3 fusion.149
  239.5 0.3 fusion.149
  241.3 0.3 fusion.149
  243.1 0.3 fusion.149
  244.8 0.3 fusion.149
  246.6 0.3 fusion.149
  247.6 5.2 %copy.124 = f32[1,1,128,128]{3,2,1,0:T(8,128)S(1)} copy(f32[1,1,128,128]{0,3,2,1:T(8,128)} %get-tuple-element.217) | data formatting | bytes 131072
  252.8 5.2 %copy.121 = f32[1,1,128,128]{3,2,1,0:T(8,128)S(1)} copy(f32[1,1,128,128]{0,3,2,1:T(8,128)} %get-tuple-element.220) | data formatting | bytes 131072
  258.1 0.9 multiply_reduce_fusion.1
  259.0 0.9 multiply_reduce_fusion.2
  261.1 38.5 %while.41 = (s32[]{:T(128)}, f32[128,128]{0,1:T(8,128)S(1)}, f32[128,128]{0,1:T(8,128)S(1)}, f32[128,128]{1,0:T(8,128)S(1)}, f32[128,128]{1,0:T(8,128)S(1)}, /*index=5*/f32[128,128]{1,0:T(8,128)S(1)}, s32[]{:T(128)}) while((s32[]{:T(128)}, f32[128,128]{0,1:T(8,128)S(1)}, f32[128,128]{0,1:T(8,128)S(1)}, f32[128,128]{1,0:T(8,128)S(1)}, ...), condition=%wide.region_8.9_spmd.clone, body=%wide.region_7.8_spmd.clone.sunk | while | flops 151273472 | bytes 2162765 | solution.py:63
  262.5 0.3 fusion.165
  302.6 0.7 maximum_bitcast_fusion
  (376 shorter events, 73.6 us)
Async XLA Ops:
  0.0 247.0 %copy-start = (f32[1,128,128]{2,1,0:T(8,128)S(1)}, f32[1,128,128]{2,1,0:T(8,128)}, u32[]{:S(2)}) copy-start(f32[1,128,128]{2,1,0:T(8,128)} %param.13) | copy-start | bytes 196612
  0.0 60.6 %copy-start.2 = (s32[256]{0:T(256)S(1)}, s32[256]{0:T(256)}, u32[]{:S(2)}) copy-start(s32[256]{0:T(256)} %param.15) | copy-start | bytes 3076
  10.5 33.4 %all-to-all-start = ((f32[16,2,1,1024]{3,1,2,0:T(2,128)}), f32[16,2,1,1024]{3,1,2,0:T(2,128)S(1)}, u32[]{:S(2)}, u32[]{:S(2)}) async-start(f32[16,2,1,1024]{3,1,2,0:T(2,128)} %constant_dynamic-update-slice_fusion), calls=%async_computation | async-start | bytes 262144 | tf_op jit(solution)/shard_map/all_to_all | solution.py:153
  44.0 7.6 %collective-permute-start.1 = (f32[2,16,1024]{2,1,0:T(8,128)S(1)}, f32[2,16,1024]{2,1,0:T(8,128)S(1)}, u32[]{:S(2)}, u32[]{:S(2)}) collective-permute-start(f32[2,16,1024]{2,1,0:T(8,128)S(1)} %bitcast.300), channel_id=1, source_target_pairs={{16,0},{17,1},{18,2},{19,3},{20,4},{21,5},{22,6},{23,7},{24,8},{25... | collective-permute-start | bytes 393224 | tf_op jit(solution)/shard_map/ppermute | solution.py:27
  45.3 7.5 %collective-permute-start = (f32[2,16,1024]{2,1,0:T(8,128)S(1)}, f32[2,16,1024]{2,1,0:T(8,128)S(1)}, u32[]{:S(2)}, u32[]{:S(2)}) collective-permute-start(f32[2,16,1024]{2,1,0:T(8,128)S(1)} %bitcast.301), channel_id=1, source_target_pairs={{0,16},{1,17},{2,18},{3,19},{4,20},{5,21},{6,22},{7,23},{8,24},{9,... | collective-permute-start | bytes 393224 | tf_op jit(solution)/shard_map/ppermute | solution.py:25
  54.8 13.4 %all-to-all-start.1 = ((f32[2,16,1024]{2,0,1:T(2,128)}), f32[2,16,1024]{2,0,1:T(2,128)S(1)}, u32[]{:S(2)}, u32[]{:S(2)}) async-start(f32[2,16,1024]{2,0,1:T(2,128)} %copy.90), calls=%async_computation.1 | async-start | bytes 262144 | tf_op jit(solution)/shard_map/all_to_all | solution.py:164
  195.3 10.5 %copy-start.1 = (f32[2,128,128]{2,1,0:T(8,128)S(1)}, f32[2,128,128]{2,1,0:T(8,128)}, u32[]{:S(2)}) copy-start(f32[2,128,128]{2,1,0:T(8,128)} %param.12) | copy-start | bytes 393220
